TPU v7x, 32 devices: a whole 2x2x4 slice. The times are simulated.
32 devices in a mesh: chan: 8 (over z, x), bl: 4 (over y, core).
Axes of the slice: x: 2, y: 2, z: 4, core: 2. Of those that a mesh axis runs over, the one named last changes fastest.
Arguments:
- visibilities: bfloat16 [1024, 1536, 2, 128], P('bl', 'chan'), may hold values from -6 to 6
- kernels: bfloat16 [64, 128, 256], replicated, may hold values from -0.1875 to 0.1875
- block_ids: int32 [4, 64, 8], P('bl'), may hold values from 0 to 255
- kernel_ids: int32 [4, 64, 8], P('bl'), may hold values from 0 to 63
- tile_counts: int32 [4, 64], P('bl'), may hold values from 1 to 8, as said below
- wedge_mask: int32 [64, 1536], P(('chan', 'bl')), may hold values 0 or 1
Outputs:
- delay_tiles: float32 [64, 2, 256, 1536], P(('chan', 'bl'))
Inputs may be any that keep to these rules, and one draw needn't show every extreme that they name: `tile_counts`: slots at or past a tile's count are ignored; in every group some tile uses all 8 slots.
All inputs are finite; a program needn't handle non-finite values. No bound on the sum of `wedge_mask` on one device may be relied on, other than what follows from the above.
Results may differ from a plain program's by a relative error of at most 0.0095.
Values may be sent and summed in bfloat16 or wider, within the bound.
No kernel may reach another device: no remote copies, remote signals or barrier semaphores. Data moves between devices by JAX's collectives and lax.ppermute only.
A program may use at most 192 MiB of HBM per device.

v0:
```python
import math
import jax
import jax.numpy as jnp
from jax import lax
from jax.sharding import PartitionSpec as P


def delay_tables(nchan):
    chans = jnp.arange(nchan, dtype=jnp.int32)
    phase = chans[:, None] * chans[None, :] % nchan
    angle = phase.astype(jnp.float32) * (2.0 * math.pi / nchan)
    return (jnp.cos(angle).astype(jnp.bfloat16), jnp.sin(angle).astype(jnp.bfloat16))


def grid_tiles(vis_blocks, kernels, list_ids, list_kernels, list_counts):
    tiles, depth = list_ids.shape
    group_size = 16
    row_count = vis_blocks.shape[1]
    cells = kernels.shape[2]
    slots = jnp.arange(depth, dtype=jnp.int32)

    def one_group(inputs):
        group_ids, group_kernels, group_counts = inputs
        keep = (slots[None, :] < group_counts[:, None]).astype(jnp.bfloat16)
        total = jnp.zeros((group_size, row_count, cells), jnp.float32)
        for slot in range(depth):
            chosen = jnp.take(vis_blocks, group_ids[:, slot], axis=0)
            weights = (
                jnp.take(kernels, group_kernels[:, slot], axis=0) * keep[:, slot][:, None, None]
            )
            total = total + jnp.einsum(
                "trs,tsx->trx", chosen, weights, preferred_element_type=jnp.float32
            )
        return total.astype(jnp.bfloat16)

    shaped = (
        list_ids.reshape(tiles // group_size, group_size, depth),
        list_kernels.reshape(tiles // group_size, group_size, depth),
        list_counts.reshape(tiles // group_size, group_size),
    )
    return lax.map(one_group, shaped)


def local(visibilities, kernels, block_ids, kernel_ids, tile_counts, wedge_mask):
    n_chan = lax.axis_size("chan")
    n_group = lax.axis_size("bl")
    nblocks = visibilities.shape[0]
    ch_dev = visibilities.shape[1]
    block_len = kernels.shape[1]
    cells = kernels.shape[2]
    vis_blocks = visibilities.reshape(nblocks, ch_dev * 2, block_len)
    list_ids = block_ids[0]
    list_kernels = kernel_ids[0]
    list_counts = tile_counts[0]
    tiles = list_ids.shape[0]
    owned = wedge_mask.shape[0]
    order = jnp.arange(tiles, dtype=jnp.int32)
    group_of = order // (n_chan * owned)
    column = order // owned % n_chan
    inner = order % owned
    source = (column * n_group + group_of) * owned + inner
    list_ids = jnp.take(list_ids, source, axis=0)
    list_kernels = jnp.take(list_kernels, source, axis=0)
    list_counts = jnp.take(list_counts, source, axis=0)
    partial_value = grid_tiles(vis_blocks, kernels, list_ids, list_kernels, list_counts)
    partial_value = partial_value.reshape(tiles, ch_dev, 2, cells)
    summed = lax.psum_scatter(partial_value, "bl", scatter_dimension=0, tiled=True).astype(
        jnp.float32
    )
    gridded = lax.all_to_all(
        summed.astype(jnp.bfloat16), "chan", split_axis=0, concat_axis=1, tiled=True
    )
    nchan = gridded.shape[1]
    cosine, sine = delay_tables(nchan)
    real_part = gridded[:, :, 0]
    imag_part = gridded[:, :, 1]
    out_real = jnp.einsum(
        "tcx,cd->txd", real_part, cosine, preferred_element_type=jnp.float32
    ) + jnp.einsum("tcx,cd->txd", imag_part, sine, preferred_element_type=jnp.float32)
    out_imag = jnp.einsum(
        "tcx,cd->txd", imag_part, cosine, preferred_element_type=jnp.float32
    ) - jnp.einsum("tcx,cd->txd", real_part, sine, preferred_element_type=jnp.float32)
    scale = 1.0 / math.sqrt(nchan)
    keep_bins = wedge_mask.astype(jnp.float32)
    return jnp.stack([out_real, out_imag], axis=1) * scale * keep_bins[:, None, None, :]


def solution(mesh):
    return jax.shard_map(
        local,
        mesh=mesh,
        in_specs=(
            P("bl", "chan", None, None),
            P(),
            P("bl", None, None),
            P("bl", None, None),
            P("bl", None),
            P(("chan", "bl"), None),
        ),
        out_specs=P(("chan", "bl"), None, None, None),
        check_vma=False,
    )
```

profile of v0, /device:TPU:0, one launch (start us, length us, event | category | flops | bytes accessed | tf_op | source)
XLA Modules:
  0.0 936.1 jit_solution(17992654445042598032)
XLA Ops:
  10.5 572.3 %while.11 = (s32[]{:T(128)}, bf16[4,16,384,256]{3,1,0,2:T(8,128)(2,1)}, s32[4,16,8]{1,2,0:T(8,128)S(1)}, bf16[256,384,128]{2,1,0:T(8,128)(2,1)}, s32[4,16,8]{1,2...) while((s32[]{:T(128)}, ...), condition=%wide.region_1.5_spmd.clone, body=%wide.region_0.4_spmd.clone.sunk | while | flops 3248506624 | bytes 160506144 | solution.py:41
  10.6 9.0 gather_fusion.2
  26.1 9.0 gather_fusion.4
  41.6 9.0 gather_fusion.6
  53.4 3.8 fusion.173
  57.2 9.0 gather_fusion.8
  69.0 3.8 fusion.174
  72.8 9.0 gather_fusion.10
  84.7 3.7 fusion.175
  88.4 9.0 gather_fusion.12
  103.8 9.0 gather_fusion
  115.7 3.8 fusion.170
  119.4 10.0 %gather_fusion.14 = bf16[16,384,128]{2,1,0:T(8,128)(2,1)} fusion(bf16[256,384,128]{2,1,0:T(8,128)(2,1)} %get-tuple-element.327, s32[1024]{0:T(1024)S(1)} %pad_clamp_fusion.48), kind=kCustom, calls=%fused_computation.10.clone.clone.1 | custom fusion | bytes 3145792 | tf_op jit(solution)/shard_map/while/body/eval_jaxpr/jit(_take)/gather | solution.py:27
  129.5 3.8 gather_fusion.15
  133.3 16.6 %fusion.177 = bf16[1,16,384,256]{3,2,1,0:T(8,128)(2,1)S(1)} fusion(f32[16,384,256]{2,1,0:T(8,128)} %fusion.170, f32[16,384,256]{2,1,0:T(8,128)} %fusion.171, f32[16,384,256]{2,1,0:T(8,128)} %fusion.172, f32[16,384,256]{2,1,0:T(8,128)} %fusion.173, f32[16,384,256]{2,1,0:T(8,128)} %fusion.174, f32[16,384,256]{2,1,0:T(8,128)} %fusion.175, ...), kind=kOutput, calls=%fused_computation.21.clone.1 | convolution fusion | flops 417071104 | bytes 49807424 | tf_op jit(solution)/shard_map/while/body/eval_jaxpr/trs,tsx->trx/dot_general | solution.py:31
  153.5 9.0 gather_fusion.2
  169.1 9.0 gather_fusion.4
  184.6 9.0 gather_fusion.6
  196.4 3.7 fusion.173
  200.2 9.0 gather_fusion.8
  212.0 3.8 fusion.174
  215.8 9.0 gather_fusion.10
  231.3 9.0 gather_fusion.12
  246.8 9.0 gather_fusion
  258.6 3.8 fusion.170
  262.4 10.0 %gather_fusion.14 = bf16[16,384,128]{2,1,0:T(8,128)(2,1)} fusion(bf16[256,384,128]{2,1,0:T(8,128)(2,1)} %get-tuple-element.327, s32[1024]{0:T(1024)S(1)} %pad_clamp_fusion.48), kind=kCustom, calls=%fused_computation.10.clone.clone.1 | custom fusion | bytes 3145792 | tf_op jit(solution)/shard_map/while/body/eval_jaxpr/jit(_take)/gather | solution.py:27
  272.5 3.8 gather_fusion.15
  276.2 16.6 %fusion.177 = bf16[1,16,384,256]{3,2,1,0:T(8,128)(2,1)S(1)} fusion(f32[16,384,256]{2,1,0:T(8,128)} %fusion.170, f32[16,384,256]{2,1,0:T(8,128)} %fusion.171, f32[16,384,256]{2,1,0:T(8,128)} %fusion.172, f32[16,384,256]{2,1,0:T(8,128)} %fusion.173, f32[16,384,256]{2,1,0:T(8,128)} %fusion.174, f32[16,384,256]{2,1,0:T(8,128)} %fusion.175, ...), kind=kOutput, calls=%fused_computation.21.clone.1 | convolution fusion | flops 417071104 | bytes 49807424 | tf_op jit(solution)/shard_map/while/body/eval_jaxpr/trs,tsx->trx/dot_general | solution.py:31
  296.5 9.0 gather_fusion.2
  312.1 9.0 gather_fusion.4
  327.6 9.0 gather_fusion.6
  339.4 3.7 fusion.173
  343.2 9.0 gather_fusion.8
  355.0 3.8 fusion.174
  358.8 9.0 gather_fusion.10
  370.6 3.7 fusion.175
  374.3 9.0 gather_fusion.12
  389.8 9.0 gather_fusion
  401.6 3.8 fusion.170
  405.4 10.0 %gather_fusion.14 = bf16[16,384,128]{2,1,0:T(8,128)(2,1)} fusion(bf16[256,384,128]{2,1,0:T(8,128)(2,1)} %get-tuple-element.327, s32[1024]{0:T(1024)S(1)} %pad_clamp_fusion.48), kind=kCustom, calls=%fused_computation.10.clone.clone.1 | custom fusion | bytes 3145792 | tf_op jit(solution)/shard_map/while/body/eval_jaxpr/jit(_take)/gather | solution.py:27
  415.5 3.8 gather_fusion.15
  419.2 16.6 %fusion.177 = bf16[1,16,384,256]{3,2,1,0:T(8,128)(2,1)S(1)} fusion(f32[16,384,256]{2,1,0:T(8,128)} %fusion.170, f32[16,384,256]{2,1,0:T(8,128)} %fusion.171, f32[16,384,256]{2,1,0:T(8,128)} %fusion.172, f32[16,384,256]{2,1,0:T(8,128)} %fusion.173, f32[16,384,256]{2,1,0:T(8,128)} %fusion.174, f32[16,384,256]{2,1,0:T(8,128)} %fusion.175, ...), kind=kOutput, calls=%fused_computation.21.clone.1 | convolution fusion | flops 417071104 | bytes 49807424 | tf_op jit(solution)/shard_map/while/body/eval_jaxpr/trs,tsx->trx/dot_general | solution.py:31
  439.5 9.0 gather_fusion.2
  455.1 9.0 gather_fusion.4
  470.6 9.0 gather_fusion.6
  482.4 3.7 fusion.173
  486.2 9.0 gather_fusion.8
  498.0 3.8 fusion.174
  501.8 9.0 gather_fusion.10
  513.6 3.7 fusion.175
  517.3 9.0 gather_fusion.12
  532.8 9.0 gather_fusion
  544.6 3.8 fusion.170
  548.4 10.0 %gather_fusion.14 = bf16[16,384,128]{2,1,0:T(8,128)(2,1)} fusion(bf16[256,384,128]{2,1,0:T(8,128)(2,1)} %get-tuple-element.327, s32[1024]{0:T(1024)S(1)} %pad_clamp_fusion.48), kind=kCustom, calls=%fused_computation.10.clone.clone.1 | custom fusion | bytes 3145792 | tf_op jit(solution)/shard_map/while/body/eval_jaxpr/jit(_take)/gather | solution.py:27
  558.5 3.8 gather_fusion.15
  562.2 16.6 %fusion.177 = bf16[1,16,384,256]{3,2,1,0:T(8,128)(2,1)S(1)} fusion(f32[16,384,256]{2,1,0:T(8,128)} %fusion.170, f32[16,384,256]{2,1,0:T(8,128)} %fusion.171, f32[16,384,256]{2,1,0:T(8,128)} %fusion.172, f32[16,384,256]{2,1,0:T(8,128)} %fusion.173, f32[16,384,256]{2,1,0:T(8,128)} %fusion.174, f32[16,384,256]{2,1,0:T(8,128)} %fusion.175, ...), kind=kOutput, calls=%fused_computation.21.clone.1 | convolution fusion | flops 417071104 | bytes 49807424 | tf_op jit(solution)/shard_map/while/body/eval_jaxpr/trs,tsx->trx/dot_general | solution.py:31
  582.8 100.0 %reduce-scatter.2.cloned.1.call-done = bf16[16,192,2,256]{3,0,2,1:T(8,128)(2,1)} async-done(((bf16[64,192,2,256]{3,0,2,1:T(8,128)(2,1)}), bf16[16,192,2,256]{3,0,2,1:T(8,128)(2,1)}) %reduce-scatter.2.cloned.1.call-update) | async-done | bytes 3145744 | tf_op jit(solution)/shard_map/reduce_scatter | solution.py:67
  682.8 6.6 copy.35
  689.4 5.6 all-to-all-start
  695.0 70.5 %all-to-all-done = bf16[16,192,2,256]{3,2,1,0:T(2,128)(2,1)S(1)} async-done(((bf16[16,192,2,256]{3,2,1,0:T(2,128)(2,1)}), bf16[16,192,2,256]{3,2,1,0:T(2,128)(2,1)S(1)}, u32[]{:S(2)}, u32[]{:S(2)}) %all-to-all-start) | async-done | bytes 3145760 | tf_op jit(solution)/shard_map/all_to_all | solution.py:70
  766.9 39.4 %fusion.77 = f32[2,256,1536]{2,1,0:T(8,128)S(1)} fusion(bf16[2,1536,256]{2,1,0:T(8,128)(2,1)S(1)} %slice_bitcast_fusion.27), kind=kOutput, calls=%fused_computation.169 | convolution fusion | flops 2439512064 | bytes 4718592 | tf_op jit(solution)/shard_map/tcx,cd->txd/dot_general | solution.py:79
  806.3 39.6 %fusion.75 = f32[2,256,1536]{2,1,0:T(8,128)S(1)} fusion(bf16[2,1536,256]{2,1,0:T(8,128)(2,1)S(1)} %slice_bitcast_fusion.26), kind=kOutput, calls=%fused_computation.168 | convolution fusion | flops 2439512064 | bytes 4718592 | tf_op jit(solution)/shard_map/tcx,cd->txd/dot_general | solution.py:82
  845.9 39.6 %fusion.92 = f32[2,1,256,1536]{3,2,0,1:T(8,128)S(1)} fusion(f32[2,256,1536]{2,1,0:T(8,128)S(1)} %fusion.77, bf16[2,1536,256]{2,1,0:T(8,128)(2,1)S(1)} %slice_bitcast_fusion.29), kind=kOutput, calls=%fused_computation.175 | convolution fusion | flops 2440298496 | bytes 7864320 | tf_op jit(solution)/shard_map/tcx,cd->txd/dot_general | solution.py:77
  885.5 39.4 %fusion.89 = f32[2,1,256,1536]{3,2,0,1:T(8,128)S(1)} fusion(f32[2,256,1536]{2,1,0:T(8,128)S(1)} %fusion.75, bf16[2,1536,256]{2,1,0:T(8,128)(2,1)S(1)} %slice_bitcast_fusion.28), kind=kOutput, calls=%fused_computation.174 | convolution fusion | flops 2440298496 | bytes 7864320 | tf_op jit(solution)/shard_map/tcx,cd->txd/dot_general | solution.py:80
  (166 shorter events, 149.9 us)
Async XLA Ops:
  6.5 3.0 copy-start
  6.5 676.3 %reduce-scatter.2.cloned.1.call-start = ((), (), s32[]{:S(2)}) async-start(), calls=%async_computation.2 | async-start | bytes 15728640 | tf_op jit(solution)/shard_map/reduce_scatter | solution.py:67
  689.4 5.6 copy-start.2
  689.4 76.2 %all-to-all-start = ((bf16[16,192,2,256]{3,2,1,0:T(2,128)(2,1)}), bf16[16,192,2,256]{3,2,1,0:T(2,128)(2,1)S(1)}, u32[]{:S(2)}, u32[]{:S(2)}) async-start(bf16[16,192,2,256]{3,2,1,0:T(2,128)(2,1)} %copy.35), calls=%async_computation.1 | async-start | bytes 6291456 | tf_op jit(solution)/shard_map/all_to_all | solution.py:70
  925.7 3.2 copy-start.1
Sparse Core Ops, SparseCore 0:
  582.9 99.8 reduce-scatter.1
where the time goes:
time: 949 us; the launch traced here: 936 us
  local copies, waits for them, and re-layouts  415 us (44%)
  matrix products  328 us (35%)
  waiting for transfers between devices  171 us (18%)
  between operations  14 us (1%)
    gather x32, local copies, waits for them, and re-layouts, one_group(): chosen = jnp.take(vis_blocks, group_ids[:, slot], axis=0)  292 us
    dot_general x32, matrix products, one_group(): jnp.einsum('trs,tsx->trx', chosen, weights, preferred_element_type=jnp.fl...  170 us
    reduce_scatter x1, waiting for transfers between devices, local(): lax.psum_scatter(partial_value, 'bl', scatter_dimension=0, tiled=True)  100 us
    gather x32, local copies, waits for them, and re-layouts, one_group(): jnp.take(kernels, group_kernels[:, slot], axis=0)  93.6 us
    all_to_all x1, waiting for transfers between devices, local(): lax.all_to_all(summed.astype(jnp.bfloat16), 'chan', split_axis=0, concat_...  70.5 us
    dot_general x1, matrix products, local(): jnp.einsum('tcx,cd->txd', real_part, cosine, preferred_element_type=jnp.f...  39.6 us
    dot_general x1, matrix products, local(): jnp.einsum('tcx,cd->txd', real_part, sine, preferred_element_type=jnp.flo...  39.6 us
    dot_general x1, matrix products, local(): jnp.einsum('tcx,cd->txd', imag_part, cosine, preferred_element_type=jnp.f...  39.4 us
  transfers between devices with their start and end apart: 2, of which 2 were waited for; matrix products, arithmetic and copies ran while one was open for 0% of the time, Pallas kernels for 0%

commit v1 on v0

--- a/solution.py
+++ b/solution.py
@@ -3,6 +3,22 @@
 import jax.numpy as jnp
 from jax import lax
 from jax.sharding import PartitionSpec as P
+
+
+def pairwise_exchange(shard, axis, split, join):
+    ways, here = (lax.axis_size(axis), lax.axis_index(axis))
+    width = shard.shape[split] // ways
+    lengths = list(shard.shape)
+    lengths[split] = width
+    height = lengths[join]
+    lengths[join] = height * ways
+    full = jnp.zeros(lengths, shard.dtype)
+    for mask in range(ways):
+        part = lax.dynamic_slice_in_dim(shard, (here ^ mask) * width, width, axis=split)
+        if mask:
+            part = lax.ppermute(part, axis, [(d, d ^ mask) for d in range(ways)])
+        full = lax.dynamic_update_slice_in_dim(full, part, (here ^ mask) * height, axis=join)
+    return full
 
 
 def delay_tables(nchan):
@@ -67,9 +83,7 @@
     summed = lax.psum_scatter(partial_value, "bl", scatter_dimension=0, tiled=True).astype(
         jnp.float32
     )
-    gridded = lax.all_to_all(
-        summed.astype(jnp.bfloat16), "chan", split_axis=0, concat_axis=1, tiled=True
-    )
+    gridded = pairwise_exchange(summed.astype(jnp.bfloat16), "chan", 0, 1)
     nchan = gridded.shape[1]
     cosine, sine = delay_tables(nchan)
     real_part = gridded[:, :, 0]

time: 949 us -> 983 us (1.036)
  the two profiles are of different devices: /device:TPU:0 before, /device:TPU:16 now
where the time goes in v1:
time: 983 us; the launch traced here: 968 us
  local copies, waits for them, and re-layouts  485 us (49%)
  matrix products  320 us (33%)
  waiting for transfers between devices  139 us (14%)
  between operations  14.1 us (1%)
    gather x32, local copies, waits for them, and re-layouts, one_group(): chosen = jnp.take(vis_blocks, group_ids[:, slot], axis=0)  292 us
    dot_general x32, matrix products, one_group(): jnp.einsum('trs,tsx->trx', chosen, weights, preferred_element_type=jnp.fl...  170 us
    reduce_scatter x1, waiting for transfers between devices, local(): lax.psum_scatter(partial_value, 'bl', scatter_dimension=0, tiled=True)  101 us
    gather x32, local copies, waits for them, and re-layouts, one_group(): jnp.take(kernels, group_kernels[:, slot], axis=0)  93.5 us
    dynamic_update_slice x8, local copies, waits for them, and re-layouts, pairwise_exchange(): lax.dynamic_update_slice_in_dim(full, part, (here ^ mask) * height, axis=...  53.7 us
    ppermute x7, waiting for transfers between devices, pairwise_exchange(): part = lax.ppermute(part, axis, [(d, d ^ mask) for d in range(ways)])  37.7 us
    dot_general x1, matrix products, local(): jnp.einsum('tcx,cd->txd', imag_part, sine, preferred_element_type=jnp.flo...  37.6 us
    dot_general x1, matrix products, local(): jnp.einsum('tcx,cd->txd', real_part, sine, preferred_element_type=jnp.flo...  37.4 us
  transfers between devices with their start and end apart: 8, of which 6 were waited for; matrix products, arithmetic and copies ran while one was open for 5% of the time, Pallas kernels for 0%

profile of v1, /device:TPU:16, one launch (start us, length us, event | category | flops | bytes accessed | tf_op | source)
XLA Modules:
  0.0 968.3 jit_solution(16106050122400893223)
XLA Ops:
  10.5 572.1 %while.11 = (s32[]{:T(128)}, bf16[4,16,384,256]{3,1,0,2:T(8,128)(2,1)}, s32[4,16,8]{1,2,0:T(8,128)S(1)}, bf16[256,384,128]{2,1,0:T(8,128)(2,1)}, s32[4,16,8]{1,2...) while((s32[]{:T(128)}, ...), condition=%wide.region_1.5_spmd.clone, body=%wide.region_0.4_spmd.clone.sunk | while | flops 3248506624 | bytes 160506144 | solution.py:57
  10.6 9.0 gather_fusion.2
  26.1 9.0 gather_fusion.4
  41.6 9.0 gather_fusion.6
  57.2 9.0 gather_fusion.8
  69.1 3.8 fusion.174
  72.8 9.0 gather_fusion.10
  88.4 9.0 gather_fusion.12
  103.9 9.0 gather_fusion
  115.7 3.8 fusion.170
  119.5 10.0 %gather_fusion.14 = bf16[16,384,128]{2,1,0:T(8,128)(2,1)} fusion(bf16[256,384,128]{2,1,0:T(8,128)(2,1)} %get-tuple-element.328, s32[1024]{0:T(1024)S(1)} %pad_clamp_fusion.48), kind=kCustom, calls=%fused_computation.10.clone.clone.1 | custom fusion | bytes 3145792 | tf_op jit(solution)/shard_map/while/body/eval_jaxpr/jit(_take)/gather | solution.py:43
  129.5 3.8 gather_fusion.15
  133.3 16.6 %fusion.177 = bf16[1,16,384,256]{3,2,1,0:T(8,128)(2,1)S(1)} fusion(f32[16,384,256]{2,1,0:T(8,128)} %fusion.170, f32[16,384,256]{2,1,0:T(8,128)} %fusion.171, f32[16,384,256]{2,1,0:T(8,128)} %fusion.172, f32[16,384,256]{2,1,0:T(8,128)} %fusion.173, f32[16,384,256]{2,1,0:T(8,128)} %fusion.174, f32[16,384,256]{2,1,0:T(8,128)} %fusion.175, ...), kind=kOutput, calls=%fused_computation.21.clone.1 | convolution fusion | flops 417071104 | bytes 49807424 | tf_op jit(solution)/shard_map/while/body/eval_jaxpr/trs,tsx->trx/dot_general | solution.py:47
  153.5 9.0 gather_fusion.2
  169.1 9.0 gather_fusion.4
  184.6 9.0 gather_fusion.6
  196.4 3.8 fusion.173
  200.2 9.0 gather_fusion.8
  212.0 3.8 fusion.174
  215.8 9.0 gather_fusion.10
  231.4 9.0 gather_fusion.12
  246.8 9.0 gather_fusion
  262.4 10.0 %gather_fusion.14 = bf16[16,384,128]{2,1,0:T(8,128)(2,1)} fusion(bf16[256,384,128]{2,1,0:T(8,128)(2,1)} %get-tuple-element.328, s32[1024]{0:T(1024)S(1)} %pad_clamp_fusion.48), kind=kCustom, calls=%fused_computation.10.clone.clone.1 | custom fusion | bytes 3145792 | tf_op jit(solution)/shard_map/while/body/eval_jaxpr/jit(_take)/gather | solution.py:43
  272.5 3.8 gather_fusion.15
  276.2 16.6 %fusion.177 = bf16[1,16,384,256]{3,2,1,0:T(8,128)(2,1)S(1)} fusion(f32[16,384,256]{2,1,0:T(8,128)} %fusion.170, f32[16,384,256]{2,1,0:T(8,128)} %fusion.171, f32[16,384,256]{2,1,0:T(8,128)} %fusion.172, f32[16,384,256]{2,1,0:T(8,128)} %fusion.173, f32[16,384,256]{2,1,0:T(8,128)} %fusion.174, f32[16,384,256]{2,1,0:T(8,128)} %fusion.175, ...), kind=kOutput, calls=%fused_computation.21.clone.1 | convolution fusion | flops 417071104 | bytes 49807424 | tf_op jit(solution)/shard_map/while/body/eval_jaxpr/trs,tsx->trx/dot_general | solution.py:47
  296.5 9.0 gather_fusion.2
  312.1 9.0 gather_fusion.4
  327.6 9.0 gather_fusion.6
  343.2 9.0 gather_fusion.8
  355.0 3.8 fusion.174
  358.8 9.0 gather_fusion.10
  374.3 9.0 gather_fusion.12
  389.8 9.0 gather_fusion
  405.4 10.0 %gather_fusion.14 = bf16[16,384,128]{2,1,0:T(8,128)(2,1)} fusion(bf16[256,384,128]{2,1,0:T(8,128)(2,1)} %get-tuple-element.328, s32[1024]{0:T(1024)S(1)} %pad_clamp_fusion.48), kind=kCustom, calls=%fused_computation.10.clone.clone.1 | custom fusion | bytes 3145792 | tf_op jit(solution)/shard_map/while/body/eval_jaxpr/jit(_take)/gather | solution.py:43
  415.5 3.8 gather_fusion.15
  419.2 16.6 %fusion.177 = bf16[1,16,384,256]{3,2,1,0:T(8,128)(2,1)S(1)} fusion(f32[16,384,256]{2,1,0:T(8,128)} %fusion.170, f32[16,384,256]{2,1,0:T(8,128)} %fusion.171, f32[16,384,256]{2,1,0:T(8,128)} %fusion.172, f32[16,384,256]{2,1,0:T(8,128)} %fusion.173, f32[16,384,256]{2,1,0:T(8,128)} %fusion.174, f32[16,384,256]{2,1,0:T(8,128)} %fusion.175, ...), kind=kOutput, calls=%fused_computation.21.clone.1 | convolution fusion | flops 417071104 | bytes 49807424 | tf_op jit(solution)/shard_map/while/body/eval_jaxpr/trs,tsx->trx/dot_general | solution.py:47
  439.5 9.0 gather_fusion.2
  455.1 9.0 gather_fusion.4
  470.6 9.0 gather_fusion.6
  486.2 9.0 gather_fusion.8
  498.0 3.8 fusion.174
  501.8 9.0 gather_fusion.10
  517.3 9.0 gather_fusion.12
  532.8 9.0 gather_fusion
  548.4 10.0 %gather_fusion.14 = bf16[16,384,128]{2,1,0:T(8,128)(2,1)} fusion(bf16[256,384,128]{2,1,0:T(8,128)(2,1)} %get-tuple-element.328, s32[1024]{0:T(1024)S(1)} %pad_clamp_fusion.48), kind=kCustom, calls=%fused_computation.10.clone.clone.1 | custom fusion | bytes 3145792 | tf_op jit(solution)/shard_map/while/body/eval_jaxpr/jit(_take)/gather | solution.py:43
  558.4 3.8 gather_fusion.15
  562.2 16.6 %fusion.177 = bf16[1,16,384,256]{3,2,1,0:T(8,128)(2,1)S(1)} fusion(f32[16,384,256]{2,1,0:T(8,128)} %fusion.170, f32[16,384,256]{2,1,0:T(8,128)} %fusion.171, f32[16,384,256]{2,1,0:T(8,128)} %fusion.172, f32[16,384,256]{2,1,0:T(8,128)} %fusion.173, f32[16,384,256]{2,1,0:T(8,128)} %fusion.174, f32[16,384,256]{2,1,0:T(8,128)} %fusion.175, ...), kind=kOutput, calls=%fused_computation.21.clone.1 | convolution fusion | flops 417071104 | bytes 49807424 | tf_op jit(solution)/shard_map/while/body/eval_jaxpr/trs,tsx->trx/dot_general | solution.py:47
  582.6 14.1 %copy.24 = bf16[64,192,2,256]{3,1,2,0:T(8,128)(2,1)} copy(bf16[64,192,2,256]{3,0,2,1:T(8,128)(2,1)} %bitcast.155) | data formatting | bytes 25165824 | tf_op jit(solution)/shard_map/reshape | solution.py:82
  596.7 101.0 %reduce-scatter.2.cloned.1.call-done = bf16[16,192,2,256]{3,1,2,0:T(8,128)(2,1)} async-done(((bf16[64,192,2,256]{3,1,2,0:T(8,128)(2,1)}), bf16[16,192,2,256]{3,1,2,0:T(8,128)(2,1)}) %reduce-scatter.2.cloned.1.call-update) | async-done | bytes 3145744 | tf_op jit(solution)/shard_map/reduce_scatter | solution.py:83
  715.4 18.7 %collective-permute-done.1 = bf16[2,192,2,256]{1,3,0,2:T(8,128)(2,1)} collective-permute-done((bf16[2,192,2,256]{1,3,0,2:T(8,128)(2,1)S(1)}, bf16[2,192,2,256]{1,3,0,2:T(8,128)(2,1)}, u32[]{:S(2)}, u32[]{:S(2)}) %collective-permute-start.1) | collective-permute-done | bytes 393248 | tf_op jit(solution)/shard_map/ppermute | solution.py:19
  736.0 6.4 dynamic_update_slice.28
  742.4 7.3 dynamic_update_slice.29
  749.6 6.0 dynamic_update_slice.30
  755.7 6.9 dynamic_update_slice.31
  762.6 6.4 dynamic_update_slice.32
  769.0 6.9 collective-permute-done.4
  775.8 7.2 dynamic_update_slice.33
  783.1 6.9 collective-permute-done.5
  790.0 6.3 dynamic_update_slice.34
  800.0 7.2 dynamic_update_slice.35
  807.7 37.6 %fusion.77 = f32[2,256,1536]{2,1,0:T(8,128)S(1)} fusion(bf16[2,1536,256]{1,2,0:T(8,128)(2,1)S(1)} %slice_bitcast_fusion.27), kind=kOutput, calls=%fused_computation.169 | convolution fusion | flops 2439512064 | bytes 4718592 | tf_op jit(solution)/shard_map/tcx,cd->txd/dot_general | solution.py:93
  845.3 37.4 %fusion.75 = f32[2,256,1536]{2,1,0:T(8,128)S(1)} fusion(bf16[2,1536,256]{1,2,0:T(8,128)(2,1)S(1)} %slice_bitcast_fusion.26), kind=kOutput, calls=%fused_computation.168 | convolution fusion | flops 2439512064 | bytes 4718592 | tf_op jit(solution)/shard_map/tcx,cd->txd/dot_general | solution.py:96
  882.7 37.2 %fusion.92 = f32[2,1,256,1536]{3,2,0,1:T(8,128)S(1)} fusion(f32[2,256,1536]{2,1,0:T(8,128)S(1)} %fusion.77, bf16[2,1536,256]{1,2,0:T(8,128)(2,1)S(1)} %slice_bitcast_fusion.29), kind=kOutput, calls=%fused_computation.175 | convolution fusion | flops 2440298496 | bytes 7864320 | tf_op jit(solution)/shard_map/tcx,cd->txd/dot_general | solution.py:91
  919.9 37.2 %fusion.89 = f32[2,1,256,1536]{3,2,0,1:T(8,128)S(1)} fusion(f32[2,256,1536]{2,1,0:T(8,128)S(1)} %fusion.75, bf16[2,1536,256]{1,2,0:T(8,128)(2,1)S(1)} %slice_bitcast_fusion.28), kind=kOutput, calls=%fused_computation.174 | convolution fusion | flops 2440298496 | bytes 7864320 | tf_op jit(solution)/shard_map/tcx,cd->txd/dot_general | solution.py:94
  (194 shorter events, 205.9 us)
Async XLA Ops:
  6.5 3.0 copy-start
  6.5 691.1 %reduce-scatter.2.cloned.1.call-start = ((), (), s32[]{:S(2)}) async-start(), calls=%async_computation.1 | async-start | bytes 15728640 | tf_op jit(solution)/shard_map/reduce_scatter | solution.py:83
  699.7 35.0 %copy-start.2 = (s32[2,1536]{1,0:T(2,128)S(1)}, s32[2,1536]{1,0:T(2,128)}, u32[]{:S(2)}) copy-start(s32[2,1536]{1,0:T(2,128)} %param.19) | copy-start | bytes 36868
  700.7 14.1 %collective-permute-start = (bf16[2,192,2,256]{1,3,0,2:T(8,128)(2,1)}, bf16[2,192,2,256]{1,3,0,2:T(8,128)(2,1)}, u32[]{:S(2)}, u32[]{:S(2)}) collective-permute-start(bf16[2,192,2,256]{1,3,0,2:T(8,128)(2,1)} %copy.37), channel_id=1, source_target_pairs={{0,4},{4,0},{8,12},{12,8},{16,20},{20,16},{24,28},{28,24},{1,5},{5... | collective-permute-start | bytes 1179656 | tf_op jit(solution)/shard_map/ppermute | solution.py:19
  702.4 31.7 %collective-permute-start.1 = (bf16[2,192,2,256]{1,3,0,2:T(8,128)(2,1)S(1)}, bf16[2,192,2,256]{1,3,0,2:T(8,128)(2,1)}, u32[]{:S(2)}, u32[]{:S(2)}) collective-permute-start(bf16[2,192,2,256]{1,3,0,2:T(8,128)(2,1)S(1)} %copy.38), channel_id=1, source_target_pairs={{0,8},{4,12},{8,0},{12,4},{16,24},{20,28},{24,16},{28,20},{1,9},{5... | collective-permute-start | bytes 1179656 | tf_op jit(solution)/shard_map/ppermute | solution.py:19
  705.0 50.7 %collective-permute-start.2 = (bf16[2,192,2,256]{1,3,0,2:T(8,128)(2,1)}, bf16[2,192,2,256]{1,3,0,2:T(8,128)(2,1)}, u32[]{:S(2)}, u32[]{:S(2)}) collective-permute-start(bf16[2,192,2,256]{1,3,0,2:T(8,128)(2,1)} %copy.39), channel_id=1, source_target_pairs={{0,12},{4,8},{8,4},{12,0},{16,28},{20,24},{24,20},{28,16},{1,13},{... | collective-permute-start | bytes 1179656 | tf_op jit(solution)/shard_map/ppermute | solution.py:19
  706.5 56.0 %collective-permute-start.3 = (bf16[2,192,2,256]{1,3,0,2:T(8,128)(2,1)}, bf16[2,192,2,256]{1,3,0,2:T(8,128)(2,1)}, u32[]{:S(2)}, u32[]{:S(2)}) collective-permute-start(bf16[2,192,2,256]{1,3,0,2:T(8,128)(2,1)} %copy.40), channel_id=1, source_target_pairs={{0,16},{4,20},{8,24},{12,28},{16,0},{20,4},{24,8},{28,12},{1,17},{... | collective-permute-start | bytes 1179656 | tf_op jit(solution)/shard_map/ppermute | solution.py:19
  708.1 67.8 %collective-permute-start.4 = (bf16[2,192,2,256]{1,3,0,2:T(8,128)(2,1)}, bf16[2,192,2,256]{1,3,0,2:T(8,128)(2,1)}, u32[]{:S(2)}, u32[]{:S(2)}) collective-permute-start(bf16[2,192,2,256]{1,3,0,2:T(8,128)(2,1)} %copy.41), channel_id=1, source_target_pairs={{0,20},{4,16},{8,28},{12,24},{16,4},{20,0},{24,12},{28,8},{1,21},{... | collective-permute-start | bytes 1179656 | tf_op jit(solution)/shard_map/ppermute | solution.py:19
  714.9 75.1 %collective-permute-start.5 = (bf16[2,192,2,256]{1,3,0,2:T(8,128)(2,1)}, bf16[2,192,2,256]{1,3,0,2:T(8,128)(2,1)}, u32[]{:S(2)}, u32[]{:S(2)}) collective-permute-start(bf16[2,192,2,256]{1,3,0,2:T(8,128)(2,1)} %copy.42), channel_id=1, source_target_pairs={{0,24},{4,28},{8,16},{12,20},{16,8},{20,12},{24,0},{28,4},{1,25},{... | collective-permute-start | bytes 1179656 | tf_op jit(solution)/shard_map/ppermute | solution.py:19
  734.1 65.9 %collective-permute-start.6 = (bf16[2,192,2,256]{1,3,0,2:T(8,128)(2,1)}, bf16[2,192,2,256]{1,3,0,2:T(8,128)(2,1)}, u32[]{:S(2)}, u32[]{:S(2)}) collective-permute-start(bf16[2,192,2,256]{1,3,0,2:T(8,128)(2,1)} %copy.43), channel_id=1, source_target_pairs={{0,28},{4,24},{8,20},{12,16},{16,12},{20,8},{24,4},{28,0},{1,29},{... | collective-permute-start | bytes 1179656 | tf_op jit(solution)/shard_map/ppermute | solution.py:19
  957.8 3.2 copy-start.1
Sparse Core Ops, SparseCore 0:
  596.8 100.8 reduce-scatter.1
